TPU v7x, 256 devices: a whole 4x4x8 slice. The times are simulated.
256 devices in a mesh: fsdp: 32 (over z, y_hi, core), dp: 8 (over y_lo, x).
Axes of the slice: x: 4, y: 4 (y_hi: 2, y_lo: 2; y = y_hi * 2 + y_lo), z: 8, core: 2. Of those that a mesh axis runs over, the one named last changes fastest.
Arguments:
- features: bfloat16 [256, 16, 16, 640], P(('fsdp', 'dp')), may hold values from -100 to 100
- weight: bfloat16 [640, 5760], P('fsdp'), may hold values from -0.078125 to 0.078125
- group_norm_gain: float32 [640], replicated, may hold values from 0.1 to 1.9
- group_norm_shift: float32 [640], replicated, may hold values from -3 to 3
- conv_bias: float32 [640], replicated, may hold values from -3 to 3
- cotangent: bfloat16 [256, 16, 16, 640], P(('fsdp', 'dp')), may hold values from -6 to 6
Outputs:
- output: bfloat16 [256, 16, 16, 640], P(('fsdp', 'dp'))
- feature_gradient: bfloat16 [256, 16, 16, 640], P(('fsdp', 'dp'))
- weight_grad: float32 [640, 5760], P('fsdp')
- gain_gradient: float32 [640], replicated
- shift_grad: float32 [640], replicated
- bias_grad: float32 [640], replicated
All inputs are finite; a program needn't handle non-finite values.
Results may differ from a plain program's by a relative error of at most 0.0044.
Values may be sent and summed in bfloat16 or wider, within the bound.
A program may use at most 128 MiB of HBM per device.

v0:
```python
import jax
import jax.numpy as jnp
from jax import lax
from jax.sharding import PartitionSpec as P

GSIZE = 40
epsilon = 1e-05


def group_average(values):
    leading = values.shape[0]
    grouped = jnp.sum(values.reshape(leading, -1, GSIZE), axis=2)
    return jnp.repeat(grouped, GSIZE, axis=1)


def apply_group_norm(features):
    widened = features.astype(jnp.float32)
    entry_count = features.shape[1] * features.shape[2] * GSIZE
    average = group_average(jnp.sum(widened, axis=(1, 2))) / entry_count
    centred = widened - average[:, None, None, :]
    spread = group_average(jnp.sum(centred * centred, axis=(1, 2))) / entry_count
    inverse_deviation = lax.rsqrt(spread + epsilon)
    return (centred * inverse_deviation[:, None, None, :], inverse_deviation, entry_count)


def spatial_pad(values):
    return jnp.pad(values, ((0, 0), (1, 1), (1, 1), (0, 0)))


def tap_window(padded, tap_index, side_len, flipped):
    row_off, col_off = divmod(tap_index, 3)
    if flipped:
        row_off, col_off = (2 - row_off, 2 - col_off)
    return padded[:, row_off : row_off + side_len, col_off : col_off + side_len, :]


def local(features, weight, group_norm_gain, group_norm_shift, conv_bias, cotangent):
    local_images = features.shape[0]
    side_len = features.shape[1]
    width_in = features.shape[3]
    width_out = cotangent.shape[3]
    images = local_images * lax.axis_size("fsdp") * lax.axis_size("dp")
    normalized_input, inverse_deviation, entry_count = apply_group_norm(features)
    preactivation = normalized_input * group_norm_gain + group_norm_shift
    hidden = jax.nn.silu(preactivation).astype(jnp.bfloat16)
    hidden_pad = spatial_pad(hidden)
    grad_pad = spatial_pad(cotangent)
    full_weight = lax.all_gather(weight, "fsdp", axis=0, tiled=True)
    conv_out = jnp.zeros((local_images, side_len, side_len, width_out), jnp.float32)
    for tap_index in range(9):
        conv_out = conv_out + jnp.einsum(
            "nijc,co->nijo",
            tap_window(hidden_pad, tap_index, side_len, False),
            full_weight[:, tap_index * width_out : (tap_index + 1) * width_out],
            preferred_element_type=jnp.float32,
        )
    output = (conv_out + conv_bias).astype(jnp.bfloat16)
    back_weight = lax.all_gather(weight, "fsdp", axis=0, tiled=True)
    grad_hidden = jnp.zeros((local_images, side_len, side_len, width_in), jnp.float32)
    for tap_index in range(9):
        grad_hidden = grad_hidden + jnp.einsum(
            "nijo,co->nijc",
            tap_window(grad_pad, tap_index, side_len, True),
            back_weight[:, tap_index * width_out : (tap_index + 1) * width_out],
            preferred_element_type=jnp.float32,
        )
    columns = []
    for tap_index in range(9):
        columns.append(
            jnp.einsum(
                "nijc,nijo->co",
                tap_window(hidden_pad, tap_index, side_len, False),
                cotangent,
                preferred_element_type=jnp.float32,
            )
        )
    local_term = jnp.concatenate(columns, axis=1)
    local_term = local_term.reshape(lax.axis_size("fsdp"), -1, 9 * width_out)
    weight_sum = lax.psum_scatter(local_term, "fsdp", scatter_dimension=0)
    weight_total = lax.psum(weight_sum.astype(jnp.float32), "dp")
    weight_grad = weight_total / images
    sigmoid = jax.nn.sigmoid(preactivation)
    preactivation_gradient = grad_hidden * sigmoid * (1.0 + preactivation * (1.0 - sigmoid))
    norm_gradient = preactivation_gradient * group_norm_gain
    first_moment = group_average(jnp.sum(norm_gradient, axis=(1, 2))) / entry_count
    second_moment = (
        group_average(jnp.sum(norm_gradient * normalized_input, axis=(1, 2))) / entry_count
    )
    feature_gradient = (
        (
            norm_gradient
            - first_moment[:, None, None, :]
            - normalized_input * second_moment[:, None, None, :]
        )
        * inverse_deviation[:, None, None, :]
    ).astype(jnp.bfloat16)
    gain_product = jnp.sum(preactivation_gradient * normalized_input, axis=(0, 1, 2))
    shift_term = jnp.sum(preactivation_gradient, axis=(0, 1, 2))
    bias_term = jnp.sum(cotangent.astype(jnp.float32), axis=(0, 1, 2))
    gain_total, shift_total, bias_total = lax.psum(
        (gain_product, shift_term, bias_term), ("fsdp", "dp")
    )
    return (
        output,
        feature_gradient,
        weight_grad,
        gain_total / images,
        shift_total / images,
        bias_total / images,
    )


def solution(mesh):
    in_specs = (
        P(("fsdp", "dp"), None, None, None),
        P("fsdp", None),
        P(),
        P(),
        P(),
        P(("fsdp", "dp"), None, None, None),
    )
    out_specs = (
        P(("fsdp", "dp"), None, None, None),
        P(("fsdp", "dp"), None, None, None),
        P("fsdp", None),
        P(),
        P(),
        P(),
    )
    return jax.shard_map(local, mesh=mesh, in_specs=in_specs, out_specs=out_specs, check_vma=False)
```

profile of v0, /device:TPU:32, one launch (start us, length us, event | category | flops | bytes accessed | tf_op | source)
XLA Modules:
  0.0 481.7 jit_solution(8834222870870780972)
XLA Ops:
  9.4 1.1 fusion.26
  10.8 105.0 %all-gather.3.cloned.1.call-done = bf16[32,20,5760]{2,1,0:T(8,128)(2,1)} async-done(((bf16[1,20,5760]{2,1,0:T(8,128)(2,1)}), bf16[32,20,5760]{2,1,0:T(8,128)(2,1)}) %all-gather.3.cloned.1.call-update) | async-done | bytes 7372816 | tf_op jit(solution)/shard_map/all_gather | solution.py:48
  115.8 9.2 %reshape.259 = bf16[640,5760]{1,0:T(8,128)(2,1)} reshape(bf16[32,20,5760]{2,1,0:T(8,128)(2,1)} %all-gather.3.cloned.1.call-done) | data formatting | bytes 14745600
  125.0 1.8 fusion.27
  126.8 2.0 convolution_add_fusion.7
  128.8 1.7 convolution_add_fusion.6
  130.5 1.6 convolution_add_fusion.5
  135.5 1.1 fusion.24
  136.6 1.6 bitcast_dynamic-update-slice_fusion.8
  138.2 1.6 bitcast_dynamic-update-slice_fusion.7
  139.9 1.6 bitcast_dynamic-update-slice_fusion.6
  141.5 1.7 bitcast_dynamic-update-slice_fusion.5
  143.2 1.6 bitcast_dynamic-update-slice_fusion.4
  144.8 1.7 bitcast_dynamic-update-slice_fusion.3
  146.5 1.6 bitcast_dynamic-update-slice_fusion.2
  148.1 1.7 bitcast_dynamic-update-slice_fusion.1
  149.8 1.6 bitcast_dynamic-update-slice_fusion
  151.4 15.2 %copy.15 = f32[640,5760]{1,0:T(8,128)} copy(f32[640,5760]{0,1:T(8,128)} %bitcast_dynamic-update-slice_fusion) | data formatting | bytes 29491200 | tf_op jit(solution)/shard_map/concatenate | solution.py:77
  166.6 13.2 %reshape.257 = f32[32,20,5760]{2,1,0:T(8,128)} reshape(f32[640,5760]{1,0:T(8,128)} %copy.15) | data formatting | bytes 29491200 | tf_op jit(solution)/shard_map/reshape | solution.py:78
  180.1 1.6 fusion.28
  181.7 1.6 convolution_add_fusion.15
  183.4 1.6 convolution_add_fusion.14
  185.0 1.6 convolution_add_fusion.13
  186.6 1.7 convolution_add_fusion.12
  188.3 1.6 convolution_add_fusion.11
  189.9 1.7 convolution_add_fusion.10
  191.6 1.7 convolution_add_fusion.9
  193.3 197.4 %reduce-scatter.4.cloned.1.call-done = f32[1,20,5760]{2,1,0:T(8,128)} async-done(((f32[32,20,5760]{2,1,0:T(8,128)}), f32[1,20,5760]{2,1,0:T(8,128)}) %reduce-scatter.4.cloned.1.call-update) | async-done | bytes 460816
  390.7 2.3 fusion.5
  393.1 76.2 %all-reduce.3 = (f32[640]{0:T(1024)S(1)}, f32[640]{0:T(1024)S(1)}, f32[640]{0:T(1024)S(1)}) all-reduce(f32[640]{0:T(1024)S(1)} %get-tuple-element.6, f32[640]{0:T(1024)S(1)} %get-tuple-element.9, f32[640]{0:T(1024)S(1)} %convert_reduce_fusion.1), channel_id=1, replica_groups=mesh['fsdp'=32,'dp'=8] {'fsdp','dp'}, use_global_device_ids=true, to_apply=%region_11.12 | all-reduce | flops 1920 | bytes 15360 | tf_op jit(solution)/shard_map/psum | solution.py:100
  470.5 2.8 all-reduce.6.cloned.1.call-done
  473.3 1.9 broadcast_multiply_fusion
  (47 shorter events, 7.4 us)
Async XLA Ops:
  7.2 108.7 %all-gather.3.cloned.1.call-start = ((), (), s32[]{:S(2)}) async-start(), calls=%async_computation.2 | async-start | bytes 9123840 | tf_op jit(solution)/shard_map/all_gather | solution.py:48
  7.9 382.8 %reduce-scatter.4.cloned.1.call-start = ((), (), s32[]{:S(2)}) async-start(), calls=%async_computation.3 | async-start | bytes 18247680
  10.8 114.2 %copy-start = (bf16[1,16,16,640]{3,2,1,0:T(8,128)(2,1)S(1)}, bf16[1,16,16,640]{3,2,1,0:T(8,128)(2,1)}, u32[]{:S(2)}) copy-start(bf16[1,16,16,640]{3,2,1,0:T(8,128)(2,1)} %param.11) | copy-start | bytes 983044
  125.0 7.1 %copy-start.1 = (bf16[640,5760]{1,0:T(8,128)(2,1)S(1)}, bf16[640,5760]{1,0:T(8,128)(2,1)}, u32[]{:S(2)}) copy-start(bf16[640,5760]{1,0:T(8,128)(2,1)} %reshape.259) | copy-start | bytes 22118404
  128.8 5.2 %copy-start.2 = (bf16[1,16,16,640]{3,2,1,0:T(8,128)(2,1)S(1)}, bf16[1,16,16,640]{3,2,1,0:T(8,128)(2,1)}, u32[]{:S(2)}) copy-start(bf16[1,16,16,640]{3,2,1,0:T(8,128)(2,1)} %param.6) | copy-start | bytes 983044
  128.8 5.2 %copy-start.3 = (f32[640]{0:T(1024)S(1)}, f32[640]{0:T(1024)}, u32[]{:S(2)}) copy-start(f32[640]{0:T(1024)} %param.8) | copy-start | bytes 7684
  128.8 5.2 %copy-start.4 = (f32[640]{0:T(1024)S(1)}, f32[640]{0:T(1024)}, u32[]{:S(2)}) copy-start(f32[640]{0:T(1024)} %param.9) | copy-start | bytes 7684
  179.8 293.5 %all-reduce.6.cloned.1.call-start = ((), (), s32[]{:S(2)}) async-start(), calls=%async_computation.1 | async-start | bytes 1105920 | tf_op jit(solution)/shard_map/psum | solution.py:80
  183.4 207.4 %copy-start.5 = (f32[640]{0:T(1024)S(1)}, f32[640]{0:T(1024)}, u32[]{:S(2)}) copy-start(f32[640]{0:T(1024)} %param.10) | copy-start | bytes 7684
Sparse Core Ops, SparseCore 0:
  10.8 105.0 all-gather.2
  180.0 210.6 reduce-scatter.3
  393.4 79.9 all-reduce.5
where the time goes:
time: 483 us; the launch traced here: 482 us
  waiting for transfers between devices  306 us (63%)
  blocking collectives  76.2 us (16%)
  matrix products  39.9 us (8%)
  local copies, waits for them, and re-layouts  38.6 us (8%)
  between operations  14 us (3%)
  other arithmetic  6.84 us (1%)
    unnamed x4, waiting for transfers between devices  198 us
    all_gather x1, waiting for transfers between devices, local(): full_weight = lax.all_gather(weight, 'fsdp', axis=0, tiled=True)  105 us
    psum x1, blocking collectives, local(): lax.psum((gain_product, shift_term, bias_term), ('fsdp', 'dp'))  76.2 us
    dot_general x9, matrix products, local(): jnp.einsum('nijc,co->nijo', tap_window(hidden_pad, tap_index, side_len, F...  15.4 us
    concatenate x1, local copies, waits for them, and re-layouts, local(): local_term = jnp.concatenate(columns, axis=1)  15.2 us
    dot_general x9, matrix products, local(): jnp.einsum('nijc,nijo->co', tap_window(hidden_pad, tap_index, side_len, F...  14.8 us
    reshape x1, local copies, waits for them, and re-layouts, local(): local_term = local_term.reshape(lax.axis_size('fsdp'), -1, 9 * width_out)  13.2 us
  transfers between devices with their start and end apart: 3, of which 3 were waited for; matrix products, arithmetic and copies ran while one was open for 4% of the time, Pallas kernels for 0%

commit v1 on v0

--- a/solution.py
+++ b/solution.py
@@ -5,6 +5,13 @@
 
 GSIZE = 40
 epsilon = 1e-05
+
+
+def exchange_gather(value, axis, along):
+    count = lax.axis_size(axis)
+    blocks = jnp.stack([value for _ in range(count)])
+    blocks = lax.all_to_all(blocks, axis, split_axis=0, concat_axis=0)
+    return jnp.concatenate(blocks, axis=along)
 
 
 def group_average(values):
@@ -45,7 +52,7 @@
     hidden = jax.nn.silu(preactivation).astype(jnp.bfloat16)
     hidden_pad = spatial_pad(hidden)
     grad_pad = spatial_pad(cotangent)
-    full_weight = lax.all_gather(weight, "fsdp", axis=0, tiled=True)
+    full_weight = exchange_gather(weight, "fsdp", 0)
     conv_out = jnp.zeros((local_images, side_len, side_len, width_out), jnp.float32)
     for tap_index in range(9):
         conv_out = conv_out + jnp.einsum(

time: 483 us -> 602 us (1.25)
  waiting for transfers between devices: 306 us -> 405 us
  local copies, waits for them, and re-layouts: 38.6 us -> 52.7 us
    all_to_all x0 -> x1, waiting for transfers between devices: none -> 236 us  [exchange_gather(): blocks = lax.all_to_all(blocks, axis, split_axis=0, concat_axis=0)]
    unnamed x4, waiting for transfers between devices: 198 us -> 61.4 us
    reshape x0 -> x1, local copies, waits for them, and re-layouts: none -> 9.24 us  [exchange_gather(): return jnp.concatenate(blocks, axis=along)]
  transfers between devices with their start and end apart: 3 -> 4, of which waited for: 3 -> 4; matrix products, arithmetic and copies ran while one was open for 4% -> 5% of each run, Pallas kernels for 0% -> 0%
where the time goes in v1:
time: 602 us; the launch traced here: 600 us
  waiting for transfers between devices  405 us (67%)
  blocking collectives  76.2 us (13%)
  local copies, waits for them, and re-layouts  52.7 us (9%)
  matrix products  39.6 us (7%)
  between operations  14 us (2%)
  other arithmetic  6.84 us (1%)
    all_to_all x1, waiting for transfers between devices, exchange_gather(): blocks = lax.all_to_all(blocks, axis, split_axis=0, concat_axis=0)  236 us
    all_gather x1, waiting for transfers between devices, local(): back_weight = lax.all_gather(weight, 'fsdp', axis=0, tiled=True)  105 us
    psum x1, blocking collectives, local(): lax.psum((gain_product, shift_term, bias_term), ('fsdp', 'dp'))  76.2 us
    unnamed x4, waiting for transfers between devices  61.4 us
    concatenate x1, local copies, waits for them, and re-layouts, local(): local_term = jnp.concatenate(columns, axis=1)  15.2 us
    dot_general x9, matrix products, local(): jnp.einsum('nijc,co->nijo', tap_window(hidden_pad, tap_index, side_len, F...  15.2 us
    dot_general x9, matrix products, local(): jnp.einsum('nijc,nijo->co', tap_window(hidden_pad, tap_index, side_len, F...  14.8 us
    reshape x1, local copies, waits for them, and re-layouts, local(): local_term = local_term.reshape(lax.axis_size('fsdp'), -1, 9 * width_out)  13.2 us
  transfers between devices with their start and end apart: 4, of which 4 were waited for; matrix products, arithmetic and copies ran while one was open for 5% of the time, Pallas kernels for 0%

profile of v1, /device:TPU:32, one launch (start us, length us, event | category | flops | bytes accessed | tf_op | source)
XLA Modules:
  0.0 600.3 jit_solution(9881854161160671474)
XLA Ops:
  10.8 105.0 %all-gather.3.cloned.1.call-done = bf16[32,20,5760]{2,1,0:T(8,128)(2,1)} async-done(((bf16[1,20,5760]{2,1,0:T(8,128)(2,1)}), bf16[32,20,5760]{2,1,0:T(8,128)(2,1)}) %all-gather.3.cloned.1.call-update) | async-done | bytes 7372816 | tf_op jit(solution)/shard_map/all_gather | solution.py:65
  115.8 9.2 %reshape.265 = bf16[640,5760]{1,0:T(8,128)(2,1)} reshape(bf16[32,20,5760]{2,1,0:T(8,128)(2,1)} %all-gather.3.cloned.1.call-done) | data formatting | bytes 14745600
  125.1 1.8 fusion.6
  126.8 2.0 convolution_add_fusion.7
  128.9 1.6 convolution_add_fusion.6
  130.5 1.6 convolution_add_fusion.5
  136.6 1.6 bitcast_dynamic-update-slice_fusion.8
  138.3 1.6 bitcast_dynamic-update-slice_fusion.7
  139.9 1.6 bitcast_dynamic-update-slice_fusion.6
  141.5 1.7 bitcast_dynamic-update-slice_fusion.5
  143.2 1.6 bitcast_dynamic-update-slice_fusion.4
  144.8 1.7 bitcast_dynamic-update-slice_fusion.3
  146.5 1.6 bitcast_dynamic-update-slice_fusion.2
  148.2 1.7 bitcast_dynamic-update-slice_fusion.1
  149.8 1.6 bitcast_dynamic-update-slice_fusion
  151.5 15.2 %copy.15 = f32[640,5760]{1,0:T(8,128)} copy(f32[640,5760]{0,1:T(8,128)} %bitcast_dynamic-update-slice_fusion) | data formatting | bytes 29491200 | tf_op jit(solution)/shard_map/concatenate | solution.py:84
  166.6 13.2 %reshape.263 = f32[32,20,5760]{2,1,0:T(8,128)} reshape(f32[640,5760]{1,0:T(8,128)} %copy.15) | data formatting | bytes 29491200 | tf_op jit(solution)/shard_map/reshape | solution.py:85
  180.8 3.9 stack.2
  184.7 5.2 all-to-all-start
  190.3 236.5 %all-to-all-done = bf16[32,20,5760]{2,1,0:T(8,128)(2,1)} async-done(((bf16[32,20,5760]{2,1,0:T(8,128)(2,1)}), bf16[32,20,5760]{2,1,0:T(8,128)(2,1)}, u32[]{:S(2)}, u32[]{:S(2)}) %all-to-all-start) | async-done | bytes 7372832 | tf_op jit(solution)/shard_map/all_to_all | solution.py:13
  426.8 9.2 %reshape.243 = bf16[640,5760]{1,0:T(8,128)(2,1)} reshape(bf16[32,20,5760]{2,1,0:T(8,128)(2,1)} %all-to-all-done) | data formatting | bytes 14745600 | tf_op jit(solution)/shard_map/reshape | solution.py:14
  436.0 1.6 fusion.7
  437.6 1.6 convolution_add_fusion.15
  439.2 1.6 convolution_add_fusion.14
  440.9 1.6 convolution_add_fusion.13
  442.5 1.6 convolution_add_fusion.12
  444.1 1.6 convolution_add_fusion.11
  448.9 60.7 %reduce-scatter.4.cloned.1.call-done = f32[1,20,5760]{2,1,0:T(8,128)} async-done(((f32[32,20,5760]{2,1,0:T(8,128)}), f32[1,20,5760]{2,1,0:T(8,128)}) %reduce-scatter.4.cloned.1.call-update) | async-done | bytes 460816
  509.6 2.3 fusion.5
  511.9 76.2 %all-reduce.3 = (f32[640]{0:T(1024)S(1)}, f32[640]{0:T(1024)S(1)}, f32[640]{0:T(1024)S(1)}) all-reduce(f32[640]{0:T(1024)S(1)} %get-tuple-element.6, f32[640]{0:T(1024)S(1)} %get-tuple-element.9, f32[640]{0:T(1024)S(1)} %convert_reduce_fusion.1), channel_id=1, replica_groups=mesh['fsdp'=32,'dp'=8] {'fsdp','dp'}, use_global_device_ids=true, to_apply=%region_11.12 | all-reduce | flops 1920 | bytes 15360 | tf_op jit(solution)/shard_map/psum | solution.py:107
  589.4 2.5 all-reduce.6.cloned.1.call-done
  591.9 1.9 broadcast_multiply_fusion
  (53 shorter events, 13.7 us)
Async XLA Ops:
  7.2 108.7 %all-gather.3.cloned.1.call-start = ((), (), s32[]{:S(2)}) async-start(), calls=%async_computation.3 | async-start | bytes 9123840 | tf_op jit(solution)/shard_map/all_gather | solution.py:65
  7.9 501.7 %reduce-scatter.4.cloned.1.call-start = ((), (), s32[]{:S(2)}) async-start(), calls=%async_computation.4 | async-start | bytes 18247680
  10.8 114.2 %copy-start = (bf16[1,16,16,640]{3,2,1,0:T(8,128)(2,1)S(1)}, bf16[1,16,16,640]{3,2,1,0:T(8,128)(2,1)}, u32[]{:S(2)}) copy-start(bf16[1,16,16,640]{3,2,1,0:T(8,128)(2,1)} %param.11) | copy-start | bytes 983044
  125.1 7.1 %copy-start.1 = (bf16[640,5760]{1,0:T(8,128)(2,1)S(1)}, bf16[640,5760]{1,0:T(8,128)(2,1)}, u32[]{:S(2)}) copy-start(bf16[640,5760]{1,0:T(8,128)(2,1)} %reshape.265) | copy-start | bytes 22118404
  128.8 5.2 copy-start.2
  128.8 5.2 copy-start.4
  128.9 5.2 copy-start.5
  179.8 1.0 copy-start.3
  184.7 242.0 %all-to-all-start = ((bf16[32,20,5760]{2,1,0:T(8,128)(2,1)}), bf16[32,20,5760]{2,1,0:T(8,128)(2,1)}, u32[]{:S(2)}, u32[]{:S(2)}) async-start(bf16[32,20,5760]{2,1,0:T(8,128)(2,1)} %stack.2), calls=%async_computation | async-start | bytes 17694720 | tf_op jit(solution)/shard_map/all_to_all | solution.py:13
  190.0 401.9 %all-reduce.6.cloned.1.call-start = ((), (), s32[]{:S(2)}) async-start(), calls=%async_computation.2 | async-start | bytes 1105920 | tf_op jit(solution)/shard_map/psum | solution.py:87
  439.2 70.4 %copy-start.6 = (f32[640]{0:T(1024)S(1)}, f32[640]{0:T(1024)}, u32[]{:S(2)}) copy-start(f32[640]{0:T(1024)} %param.10) | copy-start | bytes 7684
Sparse Core Ops, SparseCore 0:
  10.8 105.0 all-gather.2
  180.0 329.5 reduce-scatter.3
  512.2 79.6 all-reduce.5
